TPU v7x, 32 devices: a whole 2x2x4 slice. The times are simulated.
32 devices in a mesh: section: 2 (over x), seq: 4 (over z), tensor: 4 (over y, core).
Axes of the slice: x: 2, y: 2, z: 4, core: 2. Of those that a mesh axis runs over, the one named last changes fastest.
Arguments:
- q_mant: bfloat16 [2, 256, 16384], P('section', 'seq', 'tensor'), may hold values from -32 to 32
- q_scale: int32 [2, 256, 512], P('section', 'seq', 'tensor'), may hold values from -2 to 2
- key_mantissa_block: bfloat16 [2, 256, 1024], P('section', 'seq', 'tensor'), may hold values from -32 to 32
- key_exponent_scale: int32 [2, 256, 32], P('section', 'seq', 'tensor'), may hold values from -2 to 2
- value_mantissa_block: bfloat16 [2, 256, 1024], P('section', 'seq', 'tensor'), may hold values from -6 to 6
- value_exponent_scale: int32 [2, 256, 32], P('section', 'seq', 'tensor'), may hold values from -1 to 1
- cached_key_rows: bfloat16 [2, 8, 512, 128], P('section', 'tensor', 'seq'), may hold values from -12 to 12
- cached_value_rows: bfloat16 [2, 8, 512, 128], P('section', 'tensor', 'seq'), may hold values from -8 to 8
- start: int32 [2], P('section'), may hold values from 256 to 512, as said below
Outputs:
- attended: bfloat16 [2, 256, 16384], P('section', 'seq', 'tensor')
Inputs may be any that keep to these rules, and one draw needn't show every extreme that they name: The first start[s] cached positions of section s hold earlier tokens; the cache of some section is full in every draw.
All inputs are finite; a program needn't handle non-finite values.
Results may differ from a plain program's by a relative error of at most 0.0023.
Values may be sent and summed in bfloat16 or wider, within the bound.
No kernel may reach another device: no remote copies, remote signals or barrier semaphores. Data moves between devices by JAX's collectives and lax.ppermute only.
A program may use at most 64 MiB of HBM per device.

v0:
```python
import math
import jax
import jax.numpy as jnp
from jax import lax
from jax.sharding import PartitionSpec as P


def shifted(block, axis, distance):
    devices = range(lax.axis_size(axis))
    route = [((i - distance) % len(devices), i) for i in devices]
    return lax.ppermute(block, axis, route)


def decode_mantissas(mantissa, exponent):
    row_count, feature_count = mantissa.shape
    blocks = mantissa.astype(jnp.float32).reshape(row_count, feature_count // 32, 32)
    factor = jnp.exp2(exponent.astype(jnp.float32))[:, :, None]
    return (blocks * factor).reshape(row_count, feature_count).astype(jnp.bfloat16)


def attend(running, queries, section_key_rows, section_value_rows, key_start, from_cache, limit):
    head_count, tokens, head_size = queries.shape
    key_count = section_key_rows.shape[1]
    block_rows = min(512, tokens)
    inv_root = 1.0 / math.sqrt(head_size)
    key_first = jnp.asarray(key_start, jnp.int32)
    key_index = lax.iota(jnp.int32, key_count)

    def one_block(number, running):
        first_row = number * block_rows

        def update(running):
            row_max, row_total, row_sum = running
            query_block = lax.dynamic_slice_in_dim(queries, first_row, block_rows, 1)
            scores = (
                jnp.einsum(
                    "hqd,hkd->hqk",
                    query_block,
                    section_key_rows,
                    preferred_element_type=jnp.float32,
                )
                * inv_root
            )
            if from_cache:
                allowed = jnp.broadcast_to((key_index < limit)[None, None, :], scores.shape)
            else:
                query_index = first_row + lax.iota(jnp.int32, block_rows)
                allowed = jnp.broadcast_to(
                    (key_index[None, :] <= query_index[:, None])[None], scores.shape
                )
            scores = jnp.where(allowed, scores, -1e30)
            old_max = lax.dynamic_slice_in_dim(row_max, first_row, block_rows, 1)
            new_max = jnp.maximum(old_max, jnp.max(scores, axis=2))
            weights = jnp.where(allowed, jnp.exp(scores - new_max[:, :, None]), 0.0)
            factor = jnp.exp(old_max - new_max)
            old_total = lax.dynamic_slice_in_dim(row_total, first_row, block_rows, 1)
            new_total = old_total * factor + jnp.sum(weights, axis=2)
            product = jnp.einsum(
                "hqk,hkd->hqd",
                weights.astype(jnp.bfloat16),
                section_value_rows,
                preferred_element_type=jnp.float32,
            )
            old_sum = lax.dynamic_slice_in_dim(row_sum, first_row, block_rows, 1)
            new_sum = old_sum * factor[:, :, None] + product
            return (
                lax.dynamic_update_slice_in_dim(row_max, new_max, first_row, 1),
                lax.dynamic_update_slice_in_dim(row_total, new_total, first_row, 1),
                lax.dynamic_update_slice_in_dim(row_sum, new_sum, first_row, 1),
            )

        if from_cache:
            visible = key_first < limit
        else:
            visible = key_first <= first_row + block_rows - 1
        return lax.cond(visible, update, lambda unchanged: unchanged, running)

    return lax.fori_loop(0, tokens // block_rows, one_block, running)


def body(
    q_mant,
    q_scale,
    key_mantissa_block,
    key_exponent_scale,
    value_mantissa_block,
    value_exponent_scale,
    cached_key_rows,
    cached_value_rows,
    start,
):
    arrived = shifted(
        (
            q_mant[0],
            key_mantissa_block[0],
            value_mantissa_block[0],
            q_scale[0].astype(jnp.bfloat16),
            key_exponent_scale[0].astype(jnp.bfloat16),
            value_exponent_scale[0].astype(jnp.bfloat16),
        ),
        "section",
        1,
    )
    row_count = q_mant.shape[1]
    kv_here = cached_key_rows.shape[1]
    head_size = cached_key_rows.shape[3]
    queries = decode_mantissas(arrived[0], arrived[3]).reshape(row_count, -1, head_size)
    section_key_rows = decode_mantissas(arrived[1], arrived[4]).reshape(
        row_count, kv_here, head_size
    )
    section_value_rows = decode_mantissas(arrived[2], arrived[5]).reshape(
        row_count, kv_here, head_size
    )
    heads_here = queries.shape[1]
    query_group_width = heads_here // kv_here
    seq_count = lax.axis_size("seq")
    local_heads = heads_here // seq_count
    tokens = row_count * seq_count
    limit = start[0]
    mine = lax.all_to_all(queries, "seq", split_axis=1, concat_axis=0, tiled=True)
    query_block = jnp.transpose(mine, (1, 0, 2))
    running = (
        jnp.full((local_heads, tokens), -1e30, jnp.float32),
        jnp.zeros((local_heads, tokens), jnp.float32),
        jnp.zeros((local_heads, tokens, head_size), jnp.float32),
    )
    head_ids = lax.axis_index("seq") * local_heads + lax.iota(jnp.int32, local_heads)
    kv_ids = head_ids // query_group_width
    pieces = (
        lax.all_gather(cached_key_rows[0], "seq", axis=1, tiled=True),
        lax.all_gather(cached_value_rows[0], "seq", axis=1, tiled=True),
    )
    running = attend(
        running,
        query_block,
        jnp.take(pieces[0], kv_ids, axis=0),
        jnp.take(pieces[1], kv_ids, axis=0),
        jnp.int32(0),
        True,
        limit,
    )
    pieces = (
        lax.all_gather(section_key_rows, "seq", axis=0, tiled=True),
        lax.all_gather(section_value_rows, "seq", axis=0, tiled=True),
    )
    picked_keys = jnp.swapaxes(jnp.take(pieces[0], kv_ids, axis=1), 0, 1)
    picked_values = jnp.swapaxes(jnp.take(pieces[1], kv_ids, axis=1), 0, 1)
    running = attend(running, query_block, picked_keys, picked_values, jnp.int32(0), False, limit)
    row_max, row_total, row_sum = running
    finished = (row_sum / row_total[:, :, None]).astype(jnp.bfloat16)
    finished = jnp.transpose(finished, (1, 0, 2))
    returned = lax.all_to_all(finished, "seq", split_axis=0, concat_axis=1, tiled=True)
    return returned.reshape(1, row_count, heads_here * head_size)


def solution(mesh):
    return jax.shard_map(
        body,
        mesh=mesh,
        in_specs=(
            P("section", "seq", "tensor"),
            P("section", "seq", "tensor"),
            P("section", "seq", "tensor"),
            P("section", "seq", "tensor"),
            P("section", "seq", "tensor"),
            P("section", "seq", "tensor"),
            P("section", "tensor", "seq", None),
            P("section", "tensor", "seq", None),
            P("section"),
        ),
        out_specs=P("section", "seq", "tensor"),
        check_vma=False,
    )
```

profile of v0, /device:TPU:0, one launch (start us, length us, event | category | flops | bytes accessed | tf_op | source)
XLA Modules:
  0.0 120.3 jit_solution(3274771388179172553)
XLA Ops:
  0.0 3.0 %collective-permute-start = (bf16[64,4096]{1,0:T(8,128)(2,1)}, bf16[64,4096]{1,0:T(8,128)(2,1)S(1)}, u32[]{:S(2)}, u32[]{:S(2)}) collective-permute-start(bf16[64,4096]{1,0:T(8,128)(2,1)} %bitcast.60), channel_id=1, source_target_pairs={{16,0},{0,16},{17,1},{1,17},{18,2},{2,18},{19,3},{3,19},{20,4},{4,... | collective-permute-start | bytes 1572872 | tf_op jit(solution)/shard_map/ppermute | solution.py:11
  4.6 2.1 %collective-permute-start.2 = (bf16[64,256]{0,1:T(8,128)(2,1)S(1)}, bf16[64,256]{0,1:T(8,128)(2,1)S(1)}, u32[]{:S(2)}, u32[]{:S(2)}) collective-permute-start(bf16[64,256]{0,1:T(8,128)(2,1)S(1)} %bitcast.59), channel_id=1, source_target_pairs={{16,0},{0,16},{17,1},{1,17},{18,2},{2,18},{19,3},{3,19},{20,4},{4,... | collective-permute-start | bytes 98312 | tf_op jit(solution)/shard_map/ppermute | solution.py:11
  8.3 2.1 %collective-permute-start.4 = (bf16[64,256]{0,1:T(8,128)(2,1)S(1)}, bf16[64,256]{0,1:T(8,128)(2,1)S(1)}, u32[]{:S(2)}, u32[]{:S(2)}) collective-permute-start(bf16[64,256]{0,1:T(8,128)(2,1)S(1)} %bitcast.58), channel_id=1, source_target_pairs={{16,0},{0,16},{17,1},{1,17},{18,2},{2,18},{19,3},{3,19},{20,4},{4,... | collective-permute-start | bytes 98312 | tf_op jit(solution)/shard_map/ppermute | solution.py:11
  11.1 5.2 %collective-permute-done.1 = bf16[64,128]{1,0:T(8,128)(2,1)S(1)} collective-permute-done((bf16[64,128]{1,0:T(8,128)(2,1)S(1)}, bf16[64,128]{1,0:T(8,128)(2,1)S(1)}, u32[]{:S(2)}, u32[]{:S(2)}) %collective-permute-start.1) | collective-permute-done | bytes 16416 | tf_op jit(solution)/shard_map/ppermute | solution.py:11
  16.3 2.0 %collective-permute-start.5 = (bf16[64,8]{0,1:T(8,128)(2,1)S(1)}, bf16[64,8]{0,1:T(8,128)(2,1)S(1)}, u32[]{:S(2)}, u32[]{:S(2)}) collective-permute-start(bf16[64,8]{0,1:T(8,128)(2,1)S(1)} %convert_bitcast_fusion.1), channel_id=1, source_target_pairs={{16,0},{0,16},{17,1},{1,17},{18,2},{2,18},{19,3},{3,19},{20,4},{4,... | collective-permute-start | bytes 3080 | tf_op jit(solution)/shard_map/ppermute | solution.py:11
  19.2 1.1 copy.36
  20.3 4.9 %all-to-all-start = ((bf16[64,32,128]{2,0,1:T(8,128)(2,1)}), bf16[64,32,128]{2,0,1:T(8,128)(2,1)S(1)}, u32[]{:S(2)}, u32[]{:S(2)}) async-start(bf16[64,32,128]{2,0,1:T(8,128)(2,1)} %copy.36), calls=%async_computation | async-start | bytes 1048576 | tf_op jit(solution)/shard_map/all_to_all | solution.py:120
  25.2 19.9 %all-gather = bf16[1,2,512,128]{3,2,1,0:T(8,128)(2,1)S(1)} all-gather(bf16[1,2,128,128]{3,2,1,0:T(8,128)(2,1)S(1)} %copy-done.5), channel_id=2, replica_groups=mesh['section'=2,'seq'=4,'tensor'=4] {'seq'}, dimensions={2}, use_global_device_ids=true | all-gather | bytes 327680 | tf_op jit(solution)/shard_map/all_gather | solution.py:130
  45.2 13.9 %all-gather.1 = bf16[1,2,512,128]{3,2,1,0:T(8,128)(2,1)S(1)} all-gather(bf16[1,2,128,128]{3,2,1,0:T(8,128)(2,1)S(1)} %copy-done.6), channel_id=3, replica_groups=mesh['section'=2,'seq'=4,'tensor'=4] {'seq'}, dimensions={2}, use_global_device_ids=true | all-gather | bytes 327680 | tf_op jit(solution)/shard_map/all_gather | solution.py:131
  59.8 1.7 %gather_fusion.1 = bf16[8,512,128]{2,1,0:T(8,128)(2,1)} fusion(bf16[2,512,128]{2,1,0:T(8,128)(2,1)S(1)} %bitcast.50, s32[1024]{0:T(1024)S(1)} %pad_clamp_fusion), kind=kCustom, calls=%fused_computation.2.clone | custom fusion | bytes 2097184 | tf_op jit(solution)/shard_map/jit(_take)/gather | solution.py:137
  62.2 1.1 broadcast_in_dim.78
  63.4 13.6 %all_gather.14 = bf16[256,2,128]{2,0,1:T(8,128)(2,1)S(1)} all-gather(bf16[64,2,128]{2,0,1:T(8,128)(2,1)S(1)} %copy.41), channel_id=1, replica_groups=mesh['section'=2,'seq'=4,'tensor'=4] {'seq'}, dimensions={0}, use_global_device_ids=true | all-gather | bytes 163840 | tf_op jit(solution)/shard_map/all_gather | solution.py:143
  77.1 1.4 %gather_fusion.2 = bf16[8,256,128]{2,1,0:T(8,128)(2,1)} fusion(bf16[256,2,128]{2,0,1:T(8,128)(2,1)S(1)} %all_gather.14, s32[1024]{0:T(1024)S(1)} %pad_clamp_fusion), kind=kCustom, calls=%fused_computation.1.clone | custom fusion | bytes 1048608 | tf_op jit(solution)/shard_map/jit(_take)/gather | solution.py:146
  78.6 13.3 %all_gather.15 = bf16[256,2,128]{2,0,1:T(8,128)(2,1)S(1)} all-gather(bf16[64,2,128]{2,0,1:T(8,128)(2,1)S(1)} %copy.44), channel_id=1, replica_groups=mesh['section'=2,'seq'=4,'tensor'=4] {'seq'}, dimensions={0}, use_global_device_ids=true | all-gather | bytes 163840 | tf_op jit(solution)/shard_map/all_gather | solution.py:144
  92.0 1.4 %gather_fusion.3 = bf16[8,256,128]{2,1,0:T(8,128)(2,1)} fusion(bf16[256,2,128]{2,0,1:T(8,128)(2,1)S(1)} %all_gather.15, s32[1024]{0:T(1024)S(1)} %pad_clamp_fusion), kind=kCustom, calls=%fused_computation.3.clone | custom fusion | bytes 1048608 | tf_op jit(solution)/shard_map/jit(_take)/gather | solution.py:147
  93.4 1.6 %fusion.18 = (f32[8,256]{1,0:T(8,128)S(1)}, f32[8,256,256]{1,2,0:T(8,128)S(1)}) fusion(pred[256,256]{0,1:T(8,128)(4,1)S(1)} %iota_compare_fusion, bf16[8,256,128]{2,1,0:T(8,128)(2,1)S(1)} %bitcast.52, bf16[8,256,128]{2,1,0:T(8,128)(2,1)} %gather_fusion.2, pred[8]{0:T(512)(128)(4,1)S(1)} %compare_and_fusion), kind=kOutput, calls=%fused_computation.27 | convolution fusion | flops 136050688 | bytes 3219464 | tf_op jit(solution)/shard_map/while/body/eval_jaxpr/cond/branch_1_fun/hqd,hkd->hqk/dot_general | solution.py:36
  95.2 5.8 %conditional.1 = ((f32[8,256]{1,0:T(8,128)S(1)}, f32[8,256]{1,0:T(8,128)S(1)}, f32[8,256,128]{2,1,0:T(8,128)})) conditional(s32[]{:T(128)} %convert_element_type.63, (f32[8,256]{1,0:T(8,128)S(1)}, f32[8,256]{1,0:T(8,128)S(1)}, f32[8,256,128]{2,1,0:T(8,128)}) %tuple.27, (s32[]{:T(128)}, s32[512]{0:T(512)S(1)}, ...), branch_computations={%region_0.2_spmd, %region_1.5_spmd.clone} | conditional | flops 552079872 | bytes 32116872 | solution.py:76
  95.8 0.9 fusion
  96.7 1.3 %fusion.2 = f32[8,256]{1,0:T(8,128)S(1)} fusion(f32[8,256,512]{2,1,0:T(8,128)S(1)} %get-tuple-element.183, f32[8,256]{1,0:T(8,128)S(1)} %max.10, pred[512]{0:T(512)(128)(4,1)S(1)} %broadcast_compare_fusion), kind=kLoop, calls=%fused_computation.8 | loop fusion | flops 5240832 | bytes 4211200 | tf_op jit(solution)/shard_map/while/body/eval_jaxpr/cond/branch_1_fun/reduce_sum | solution.py:57
  98.3 1.7 %fusion.6 = f32[8,256,128]{2,1,0:T(8,128)S(1)} fusion(f32[8,256,512]{2,1,0:T(8,128)S(1)} %get-tuple-element.183, f32[8,256]{1,0:T(8,128)S(1)} %max.10, pred[512]{0:T(512)(128)(4,1)S(1)} %broadcast_compare_fusion, bf16[8,512,128]{2,1,0:T(8,128)(2,1)S(1)} %copy-done, bf16[8,512,128]{2,1,0:T(8,128)(2,1)S(1)} %get-tuple-element.164, ...), kind=kOutput, calls=%fused_computation.11 | convolution fusion | flops 274726912 | bytes 8405512 | tf_op jit(solution)/shard_map/while/body/eval_jaxpr/cond/branch_1_fun/hqk,hkd->hqd/dot_general | solution.py:58
  100.0 1.0 copy-done.2
  102.3 1.4 %fusion.23 = bf16[256,8,128]{2,0,1:T(8,128)(2,1)S(1)} fusion(f32[8,256,256]{1,2,0:T(8,128)S(1)} %get-tuple-element.185, f32[8,256]{1,0:T(8,128)S(1)} %max.9, f32[8,256,128]{2,1,0:T(8,128)S(1)} %copy-done.3, pred[256,256]{0,1:T(8,128)(4,1)S(1)} %iota_compare_fusion, bf16[8,256,128]{2,1,0:T(8,128)(2,1)S(1)} %copy-done.4, ...), kind=kOutput, calls=%fused_computation.33 | convolution fusion | flops 138149888 | bytes 4284424 | tf_op jit(solution)/shard_map/while/body/eval_jaxpr/cond/branch_1_fun/hqk,hkd->hqd/dot_general | solution.py:58
  104.1 15.0 %all_to_all.33 = bf16[256,8,128]{2,1,0:T(8,128)(2,1)S(1)} all-to-all(bf16[256,8,128]{2,1,0:T(8,128)(2,1)S(1)} %copy.46), channel_id=1, replica_groups=mesh['section'=2,'seq'=4,'tensor'=4] {'seq'}, dimensions={0} | all-to-all | bytes 1048576 | tf_op jit(solution)/shard_map/all_to_all | solution.py:152
  119.3 1.0 reshape.69
  (55 shorter events, 8.6 us)
Async XLA Ops:
  0.0 18.4 %collective-permute-start = (bf16[64,4096]{1,0:T(8,128)(2,1)}, bf16[64,4096]{1,0:T(8,128)(2,1)S(1)}, u32[]{:S(2)}, u32[]{:S(2)}) collective-permute-start(bf16[64,4096]{1,0:T(8,128)(2,1)} %bitcast.60), channel_id=1, source_target_pairs={{16,0},{0,16},{17,1},{1,17},{18,2},{2,18},{19,3},{3,19},{20,4},{4,... | collective-permute-start | bytes 1572872 | tf_op jit(solution)/shard_map/ppermute | solution.py:11
  3.7 12.6 %collective-permute-start.1 = (bf16[64,128]{1,0:T(8,128)(2,1)S(1)}, bf16[64,128]{1,0:T(8,128)(2,1)S(1)}, u32[]{:S(2)}, u32[]{:S(2)}) collective-permute-start(bf16[64,128]{1,0:T(8,128)(2,1)S(1)} %convert_bitcast_fusion), channel_id=1, source_target_pairs={{16,0},{0,16},{17,1},{1,17},{18,2},{2,18},{19,3},{3,19},{20,4},{4,... | collective-permute-start | bytes 49160 | tf_op jit(solution)/shard_map/ppermute | solution.py:11
  4.6 58.7 %collective-permute-start.2 = (bf16[64,256]{0,1:T(8,128)(2,1)S(1)}, bf16[64,256]{0,1:T(8,128)(2,1)S(1)}, u32[]{:S(2)}, u32[]{:S(2)}) collective-permute-start(bf16[64,256]{0,1:T(8,128)(2,1)S(1)} %bitcast.59), channel_id=1, source_target_pairs={{16,0},{0,16},{17,1},{1,17},{18,2},{2,18},{19,3},{3,19},{20,4},{4,... | collective-permute-start | bytes 98312 | tf_op jit(solution)/shard_map/ppermute | solution.py:11
  7.4 55.9 %collective-permute-start.3 = (bf16[64,8]{0,1:T(8,128)(2,1)S(1)}, bf16[64,8]{0,1:T(8,128)(2,1)S(1)}, u32[]{:S(2)}, u32[]{:S(2)}) collective-permute-start(bf16[64,8]{0,1:T(8,128)(2,1)S(1)} %convert_bitcast_fusion.2), channel_id=1, source_target_pairs={{16,0},{0,16},{17,1},{1,17},{18,2},{2,18},{19,3},{3,19},{20,4},{4,... | collective-permute-start | bytes 3080 | tf_op jit(solution)/shard_map/ppermute | solution.py:11
  8.3 70.2 %collective-permute-start.4 = (bf16[64,256]{0,1:T(8,128)(2,1)S(1)}, bf16[64,256]{0,1:T(8,128)(2,1)S(1)}, u32[]{:S(2)}, u32[]{:S(2)}) collective-permute-start(bf16[64,256]{0,1:T(8,128)(2,1)S(1)} %bitcast.58), channel_id=1, source_target_pairs={{16,0},{0,16},{17,1},{1,17},{18,2},{2,18},{19,3},{3,19},{20,4},{4,... | collective-permute-start | bytes 98312 | tf_op jit(solution)/shard_map/ppermute | solution.py:11
  16.3 47.0 %collective-permute-start.5 = (bf16[64,8]{0,1:T(8,128)(2,1)S(1)}, bf16[64,8]{0,1:T(8,128)(2,1)S(1)}, u32[]{:S(2)}, u32[]{:S(2)}) collective-permute-start(bf16[64,8]{0,1:T(8,128)(2,1)S(1)} %convert_bitcast_fusion.1), channel_id=1, source_target_pairs={{16,0},{0,16},{17,1},{1,17},{18,2},{2,18},{19,3},{3,19},{20,4},{4,... | collective-permute-start | bytes 3080 | tf_op jit(solution)/shard_map/ppermute | solution.py:11
  18.9 6.2 %copy-start.5 = (bf16[1,2,128,128]{3,2,1,0:T(8,128)(2,1)S(1)}, bf16[1,2,128,128]{3,2,1,0:T(8,128)(2,1)}, u32[]{:S(2)}) copy-start(bf16[1,2,128,128]{3,2,1,0:T(8,128)(2,1)} %param.21) | copy-start | bytes 196612
  18.9 26.2 %copy-start.6 = (bf16[1,2,128,128]{3,2,1,0:T(8,128)(2,1)S(1)}, bf16[1,2,128,128]{3,2,1,0:T(8,128)(2,1)}, u32[]{:S(2)}) copy-start(bf16[1,2,128,128]{3,2,1,0:T(8,128)(2,1)} %param.22) | copy-start | bytes 196612
  20.3 73.1 %all-to-all-start = ((bf16[64,32,128]{2,0,1:T(8,128)(2,1)}), bf16[64,32,128]{2,0,1:T(8,128)(2,1)S(1)}, u32[]{:S(2)}, u32[]{:S(2)}) async-start(bf16[64,32,128]{2,0,1:T(8,128)(2,1)} %copy.36), calls=%async_computation | async-start | bytes 1048576 | tf_op jit(solution)/shard_map/all_to_all | solution.py:120
  96.7 1.3 %copy-start = (bf16[8,512,128]{2,1,0:T(8,128)(2,1)S(1)}, bf16[8,512,128]{2,1,0:T(8,128)(2,1)}, u32[]{:S(2)}) copy-start(bf16[8,512,128]{2,1,0:T(8,128)(2,1)} %get-tuple-element.165) | copy-start | bytes 3145732 | tf_op jit(solution)/shard_map/while/body/eval_jaxpr/cond
  96.7 1.5 %copy-start.1 = (f32[8,256,128]{2,1,0:T(8,128)S(1)}, f32[8,256,128]{2,1,0:T(8,128)}, u32[]{:S(2)}) copy-start(f32[8,256,128]{2,1,0:T(8,128)} %get-tuple-element.162) | copy-start | bytes 3145732 | tf_op jit(solution)/shard_map/while/body/eval_jaxpr/cond
  100.0 1.0 copy-start.2
  101.0 1.2 %copy-start.3 = (f32[8,256,128]{2,1,0:T(8,128)S(1)}, f32[8,256,128]{2,1,0:T(8,128)}, u32[]{:S(2)}) copy-start(f32[8,256,128]{2,1,0:T(8,128)} %get-tuple-element.147) | copy-start | bytes 3145732
  101.0 1.4 %copy-start.4 = (bf16[8,256,128]{2,1,0:T(8,128)(2,1)S(1)}, bf16[8,256,128]{2,1,0:T(8,128)(2,1)}, u32[]{:S(2)}) copy-start(bf16[8,256,128]{2,1,0:T(8,128)(2,1)} %gather_fusion.3) | copy-start | bytes 1572868
where the time goes:
time: 121 us; the launch traced here: 120 us
  blocking collectives  75.9 us (63%)
  starting transfers between devices  14 us (12%)
  local copies, waits for them, and re-layouts  13.7 us (11%)
  matrix products  5.59 us (5%)
  waiting for transfers between devices  5.23 us (4%)
  other arithmetic  4.94 us (4%)
    all_gather x1, blocking collectives, body(): lax.all_gather(cached_key_rows[0], 'seq', axis=1, tiled=True)  19.9 us
    all_to_all x1, blocking collectives, body(): lax.all_to_all(finished, 'seq', split_axis=0, concat_axis=1, tiled=True)  15 us
    all_gather x1, blocking collectives, body(): lax.all_gather(cached_value_rows[0], 'seq', axis=1, tiled=True)  13.9 us
    all_gather x1, blocking collectives, body(): lax.all_gather(section_key_rows, 'seq', axis=0, tiled=True)  13.6 us
    all_gather x1, blocking collectives, body(): lax.all_gather(section_value_rows, 'seq', axis=0, tiled=True)  13.3 us
    ppermute x6, starting transfers between devices, shifted(): return lax.ppermute(block, axis, route)  9.17 us
    ppermute x6, waiting for transfers between devices, shifted(): return lax.ppermute(block, axis, route)  5.23 us
    all_to_all x1, starting transfers between devices, body(): lax.all_to_all(queries, 'seq', split_axis=1, concat_axis=0, tiled=True)  4.87 us
  transfers between devices with their start and end apart: 7, of which 1 were waited for; matrix products, arithmetic and copies ran while one was open for 10% of the time, Pallas kernels for 0%

commit v1 on v0

--- a/solution.py
+++ b/solution.py
@@ -1,8 +1,33 @@
+import functools
 import math
 import jax
 import jax.numpy as jnp
 from jax import lax
 from jax.sharding import PartitionSpec as P
+
+
+def streams_create(z_in, axis_name):
+    local_part, placed = (lax.axis_size(axis_name), lax.axis_index(axis_name))
+    v_now = z_in.shape[0] // local_part
+    r_now = list(z_in.shape)
+    r_now[0] = v_now
+    block_next = r_now[1]
+    r_now[1] = block_next * local_part
+    shaped = jnp.zeros(r_now, z_in.dtype)
+    for src_i in range(local_part):
+        side_arr = lax.dynamic_slice_in_dim(z_in, (placed ^ src_i) * v_now, v_now, axis=0)
+        if src_i:
+            lanes = []
+            for nth in range(local_part):
+                lanes.append((nth, nth ^ src_i))
+            side_arr = lax.ppermute(side_arr, axis_name=axis_name, perm=lanes)
+        shaped = lax.dynamic_update_slice_in_dim(
+            shaped, side_arr, (placed ^ src_i) * block_next, axis=1
+        )
+    return shaped
+
+
+touch_the_local_data = functools.partial(streams_create, axis_name="seq")
 
 
 def shifted(block, axis, distance):
@@ -149,7 +174,7 @@
     row_max, row_total, row_sum = running
     finished = (row_sum / row_total[:, :, None]).astype(jnp.bfloat16)
     finished = jnp.transpose(finished, (1, 0, 2))
-    returned = lax.all_to_all(finished, "seq", split_axis=0, concat_axis=1, tiled=True)
+    returned = touch_the_local_data(finished)
     return returned.reshape(1, row_count, heads_here * head_size)
 
 

time: 121 us -> 108 us (0.89)
  blocking collectives: 75.9 us -> 59.6 us
  starting transfers between devices: 14 us -> 16.7 us
  local copies, waits for them, and re-layouts: 13.7 us -> 15.5 us
    all_to_all x1 -> x0, blocking collectives: 15 us -> none  [body(): lax.all_to_all(finished, 'seq', split_axis=0, concat_axis=1, tiled=True)]
    all_gather x1, blocking collectives: 19.9 us -> 14.4 us  [body(): lax.all_gather(cached_key_rows[0], 'seq', axis=1, tiled=True)]
    ppermute x6, waiting for transfers between devices: 5.23 us -> 0.02 us  [shifted(): return lax.ppermute(block, axis, route)]
    all_gather x1, blocking collectives: 13.9 us -> 18.4 us  [body(): lax.all_gather(cached_value_rows[0], 'seq', axis=1, tiled=True)]
    ppermute x0 -> x3, starting transfers between devices: none -> 4.45 us  [streams_create(): side_arr = lax.ppermute(side_arr, axis_name=axis_name, perm=lanes)]
    ppermute x0 -> x3, waiting for transfers between devices: none -> 4.32 us  [streams_create(): side_arr = lax.ppermute(side_arr, axis_name=axis_name, perm=lanes)]
    ppermute x6, starting transfers between devices: 9.17 us -> 7.69 us  [shifted(): return lax.ppermute(block, axis, route)]
    dynamic_update_slice x0 -> x5, local copies, waits for them, and re-layouts: none -> 1.43 us  [streams_create(): lax.dynamic_update_slice_in_dim(shaped, side_arr, (placed ^ src_i) * bloc...]
  transfers between devices with their start and end apart: 7 -> 10, of which waited for: 1 -> 2; matrix products, arithmetic and copies ran while one was open for 10% -> 13% of each run, Pallas kernels for 0% -> 0%
where the time goes in v1:
time: 108 us
  blocking collectives  59.6 us (55%)
  starting transfers between devices  16.7 us (15%)
  local copies, waits for them, and re-layouts  15.5 us (14%)
  matrix products  5.6 us (5%)
  other arithmetic  4.93 us (5%)
  waiting for transfers between devices  4.34 us (4%)
    all_gather x1, blocking collectives, body(): lax.all_gather(cached_value_rows[0], 'seq', axis=1, tiled=True)  18.4 us
    all_gather x1, blocking collectives, body(): lax.all_gather(cached_key_rows[0], 'seq', axis=1, tiled=True)  14.4 us
    all_gather x1, blocking collectives, body(): lax.all_gather(section_key_rows, 'seq', axis=0, tiled=True)  13.3 us
    all_gather x1, blocking collectives, body(): lax.all_gather(section_value_rows, 'seq', axis=0, tiled=True)  13.3 us
    ppermute x6, starting transfers between devices, shifted(): return lax.ppermute(block, axis, route)  7.69 us
    all_to_all x1, starting transfers between devices, body(): lax.all_to_all(queries, 'seq', split_axis=1, concat_axis=0, tiled=True)  4.52 us
    ppermute x3, starting transfers between devices, streams_create(): side_arr = lax.ppermute(side_arr, axis_name=axis_name, perm=lanes)  4.45 us
    ppermute x3, waiting for transfers between devices, streams_create(): side_arr = lax.ppermute(side_arr, axis_name=axis_name, perm=lanes)  4.32 us
  transfers between devices with their start and end apart: 10, of which 2 were waited for; matrix products, arithmetic and copies ran while one was open for 13% of the time, Pallas kernels for 0%

profile of v1, /device:TPU:0, one launch (start us, length us, event | category | flops | bytes accessed | tf_op | source)
XLA Modules:
  0.0 107.6 jit_solution(7129141240492421645)
XLA Ops:
  0.0 3.0 %collective-permute-start = (bf16[64,4096]{1,0:T(8,128)(2,1)}, bf16[64,4096]{1,0:T(8,128)(2,1)S(1)}, u32[]{:S(2)}, u32[]{:S(2)}) collective-permute-start(bf16[64,4096]{1,0:T(8,128)(2,1)} %bitcast.60), channel_id=1, source_target_pairs={{16,0},{0,16},{17,1},{1,17},{18,2},{2,18},{19,3},{3,19},{20,4},{4,... | collective-permute-start | bytes 1572872 | tf_op jit(solution)/shard_map/ppermute | solution.py:36
  4.6 2.1 %collective-permute-start.2 = (bf16[64,256]{0,1:T(8,128)(2,1)S(1)}, bf16[64,256]{0,1:T(8,128)(2,1)S(1)}, u32[]{:S(2)}, u32[]{:S(2)}) collective-permute-start(bf16[64,256]{0,1:T(8,128)(2,1)S(1)} %bitcast.59), channel_id=1, source_target_pairs={{16,0},{0,16},{17,1},{1,17},{18,2},{2,18},{19,3},{3,19},{20,4},{4,... | collective-permute-start | bytes 98312 | tf_op jit(solution)/shard_map/ppermute | solution.py:36
  8.3 2.1 %collective-permute-start.4 = (bf16[64,256]{0,1:T(8,128)(2,1)S(1)}, bf16[64,256]{0,1:T(8,128)(2,1)S(1)}, u32[]{:S(2)}, u32[]{:S(2)}) collective-permute-start(bf16[64,256]{0,1:T(8,128)(2,1)S(1)} %bitcast.58), channel_id=1, source_target_pairs={{16,0},{0,16},{17,1},{1,17},{18,2},{2,18},{19,3},{3,19},{20,4},{4,... | collective-permute-start | bytes 98312 | tf_op jit(solution)/shard_map/ppermute | solution.py:36
  11.1 14.4 %all-gather = bf16[1,2,512,128]{3,2,1,0:T(8,128)(2,1)S(1)} all-gather(bf16[1,2,128,128]{3,2,1,0:T(8,128)(2,1)} %param.21), channel_id=2, replica_groups=mesh['section'=2,'seq'=4,'tensor'=4] {'seq'}, dimensions={2}, use_global_device_ids=true | all-gather | bytes 327680 | tf_op jit(solution)/shard_map/all_gather | solution.py:155
  26.9 1.1 %copy.39 = bf16[64,32,128]{2,0,1:T(8,128)(2,1)} copy(bf16[64,32,128]{0,2,1:T(8,128)(2,1)S(1)} %bitcast.52) | data formatting | bytes 1048576 | tf_op jit(solution)/shard_map/reshape | solution.py:132
  28.0 4.5 %all-to-all-start = ((bf16[64,32,128]{2,0,1:T(8,128)(2,1)}), bf16[64,32,128]{2,0,1:T(8,128)(2,1)S(1)}, u32[]{:S(2)}, u32[]{:S(2)}) async-start(bf16[64,32,128]{2,0,1:T(8,128)(2,1)} %copy.39), calls=%async_computation | async-start | bytes 1048576 | tf_op jit(solution)/shard_map/all_to_all | solution.py:145
  32.5 18.4 %all-gather.1 = bf16[1,2,512,128]{3,2,1,0:T(8,128)(2,1)S(1)} all-gather(bf16[1,2,128,128]{3,2,1,0:T(8,128)(2,1)S(1)} %copy-done.6), channel_id=3, replica_groups=mesh['section'=2,'seq'=4,'tensor'=4] {'seq'}, dimensions={2}, use_global_device_ids=true | all-gather | bytes 327680 | tf_op jit(solution)/shard_map/all_gather | solution.py:156
  51.8 1.7 %gather_fusion.1 = bf16[8,512,128]{2,1,0:T(8,128)(2,1)} fusion(bf16[2,512,128]{2,1,0:T(8,128)(2,1)S(1)} %bitcast.51, s32[1024]{0:T(1024)S(1)} %pad_clamp_fusion), kind=kCustom, calls=%fused_computation.2.clone | custom fusion | bytes 2097184 | tf_op jit(solution)/shard_map/jit(_take)/gather | solution.py:162
  54.1 1.1 %broadcast_in_dim.82 = f32[8,256,128]{2,1,0:T(8,128)} broadcast(f32[]{:T(128)} %constant.70.clone.1), dimensions={} | broadcast | bytes 1048580 | tf_op jit(solution)/shard_map/broadcast_in_dim | solution.py:150
  55.4 13.3 %all_gather.14 = bf16[256,2,128]{2,0,1:T(8,128)(2,1)S(1)} all-gather(bf16[64,2,128]{2,0,1:T(8,128)(2,1)S(1)} %copy.44), channel_id=1, replica_groups=mesh['section'=2,'seq'=4,'tensor'=4] {'seq'}, dimensions={0}, use_global_device_ids=true | all-gather | bytes 163840 | tf_op jit(solution)/shard_map/all_gather | solution.py:168
  68.7 1.4 %gather_fusion.2 = bf16[8,256,128]{2,1,0:T(8,128)(2,1)} fusion(bf16[256,2,128]{2,0,1:T(8,128)(2,1)S(1)} %all_gather.14, s32[1024]{0:T(1024)S(1)} %pad_clamp_fusion), kind=kCustom, calls=%fused_computation.1.clone | custom fusion | bytes 1048608 | tf_op jit(solution)/shard_map/jit(_take)/gather | solution.py:171
  70.3 13.3 %all_gather.15 = bf16[256,2,128]{2,0,1:T(8,128)(2,1)S(1)} all-gather(bf16[64,2,128]{2,0,1:T(8,128)(2,1)S(1)} %copy.47), channel_id=1, replica_groups=mesh['section'=2,'seq'=4,'tensor'=4] {'seq'}, dimensions={0}, use_global_device_ids=true | all-gather | bytes 163840 | tf_op jit(solution)/shard_map/all_gather | solution.py:169
  83.6 1.4 %gather_fusion.3 = bf16[8,256,128]{2,1,0:T(8,128)(2,1)} fusion(bf16[256,2,128]{2,0,1:T(8,128)(2,1)S(1)} %all_gather.15, s32[1024]{0:T(1024)S(1)} %pad_clamp_fusion), kind=kCustom, calls=%fused_computation.3.clone | custom fusion | bytes 1048608 | tf_op jit(solution)/shard_map/jit(_take)/gather | solution.py:172
  85.1 1.6 %fusion.18 = (f32[8,256]{1,0:T(8,128)S(1)}, f32[8,256,256]{1,2,0:T(8,128)S(1)}) fusion(pred[256,256]{0,1:T(8,128)(4,1)S(1)} %iota_compare_fusion, bf16[8,256,128]{2,1,0:T(8,128)(2,1)S(1)} %bitcast.53, bf16[8,256,128]{2,1,0:T(8,128)(2,1)} %gather_fusion.2, pred[8]{0:T(512)(128)(4,1)S(1)} %compare_and_fusion), kind=kOutput, calls=%fused_computation.27 | convolution fusion | flops 136050688 | bytes 3219464 | tf_op jit(solution)/shard_map/while/body/eval_jaxpr/cond/branch_1_fun/hqd,hkd->hqk/dot_general | solution.py:61
  86.8 5.8 %conditional.1 = ((f32[8,256]{1,0:T(8,128)S(1)}, f32[8,256]{1,0:T(8,128)S(1)}, f32[8,256,128]{2,1,0:T(8,128)})) conditional(s32[]{:T(128)} %convert_element_type.63, (f32[8,256]{1,0:T(8,128)S(1)}, f32[8,256]{1,0:T(8,128)S(1)}, f32[8,256,128]{2,1,0:T(8,128)}) %tuple.27, (s32[]{:T(128)}, s32[512]{0:T(512)S(1)}, ...), branch_computations={%region_0.2_spmd, %region_1.5_spmd.clone} | conditional | flops 552079872 | bytes 32116872 | solution.py:101
  88.4 1.3 %fusion.2 = f32[8,256]{1,0:T(8,128)S(1)} fusion(f32[8,256,512]{2,1,0:T(8,128)S(1)} %get-tuple-element.183, f32[8,256]{1,0:T(8,128)S(1)} %max.10, pred[512]{0:T(512)(128)(4,1)S(1)} %broadcast_compare_fusion), kind=kLoop, calls=%fused_computation.8 | loop fusion | flops 5240832 | bytes 4211200 | tf_op jit(solution)/shard_map/while/body/eval_jaxpr/cond/branch_1_fun/reduce_sum | solution.py:82
  89.9 1.7 %fusion.6 = f32[8,256,128]{2,1,0:T(8,128)S(1)} fusion(f32[8,256,512]{2,1,0:T(8,128)S(1)} %get-tuple-element.183, f32[8,256]{1,0:T(8,128)S(1)} %max.10, pred[512]{0:T(512)(128)(4,1)S(1)} %broadcast_compare_fusion, bf16[8,512,128]{2,1,0:T(8,128)(2,1)S(1)} %copy-done, bf16[8,512,128]{2,1,0:T(8,128)(2,1)S(1)} %get-tuple-element.164, ...), kind=kOutput, calls=%fused_computation.11 | convolution fusion | flops 274726912 | bytes 8405512 | tf_op jit(solution)/shard_map/while/body/eval_jaxpr/cond/branch_1_fun/hqk,hkd->hqd/dot_general | solution.py:83
  91.6 1.0 copy-done.2
  94.0 1.4 %fusion.22 = bf16[8,256,128]{2,1,0:T(8,128)(2,1)S(1)} fusion(f32[8,256,256]{1,2,0:T(8,128)S(1)} %get-tuple-element.188, f32[8,256]{1,0:T(8,128)S(1)} %max.9, f32[8,256,128]{2,1,0:T(8,128)S(1)} %copy-done.3, pred[256,256]{0,1:T(8,128)(4,1)S(1)} %iota_compare_fusion, bf16[8,256,128]{2,1,0:T(8,128)(2,1)S(1)} %copy-done.5, ...), kind=kOutput, calls=%fused_computation.32 | convolution fusion | flops 138149888 | bytes 4284424 | tf_op jit(solution)/shard_map/while/body/eval_jaxpr/cond/branch_1_fun/hqk,hkd->hqd/dot_general | solution.py:83
  97.2 2.4 %collective-permute-start.7 = (bf16[64,8,128]{2,0,1:T(8,128)(2,1)S(1)}, bf16[64,8,128]{2,0,1:T(8,128)(2,1)S(1)}, u32[]{:S(2)}, u32[]{:S(2)}) collective-permute-start(bf16[64,8,128]{2,0,1:T(8,128)(2,1)S(1)} %get-tuple-element.185), channel_id=1, source_target_pairs={{0,8},{4,12},{8,0},{12,4},{1,9},{5,13},{9,1},{13,5},{2,10},{6,14},... | collective-permute-start | bytes 393224 | tf_op jit(solution)/shard_map/ppermute | solution.py:23
  99.6 1.1 %collective-permute-start.8 = (bf16[64,8,128]{2,0,1:T(8,128)(2,1)S(1)}, bf16[64,8,128]{2,0,1:T(8,128)(2,1)S(1)}, u32[]{:S(2)}, u32[]{:S(2)}) collective-permute-start(bf16[64,8,128]{2,0,1:T(8,128)(2,1)S(1)} %get-tuple-element.184), channel_id=1, source_target_pairs={{0,12},{4,8},{8,4},{12,0},{1,13},{5,9},{9,5},{13,1},{2,14},{6,10},... | collective-permute-start | bytes 393224 | tf_op jit(solution)/shard_map/ppermute | solution.py:23
  101.8 2.7 %collective-permute-done.7 = bf16[64,8,128]{2,0,1:T(8,128)(2,1)S(1)} collective-permute-done((bf16[64,8,128]{2,0,1:T(8,128)(2,1)S(1)}, bf16[64,8,128]{2,0,1:T(8,128)(2,1)S(1)}, u32[]{:S(2)}, u32[]{:S(2)}) %collective-permute-start.7) | collective-permute-done | bytes 131104 | tf_op jit(solution)/shard_map/ppermute | solution.py:23
  104.9 1.6 %collective-permute-done.8 = bf16[64,8,128]{2,0,1:T(8,128)(2,1)S(1)} collective-permute-done((bf16[64,8,128]{2,0,1:T(8,128)(2,1)S(1)}, bf16[64,8,128]{2,0,1:T(8,128)(2,1)S(1)}, u32[]{:S(2)}, u32[]{:S(2)}) %collective-permute-start.8) | collective-permute-done | bytes 131104 | tf_op jit(solution)/shard_map/ppermute | solution.py:23
  106.6 1.0 reshape.68
  (65 shorter events, 12.9 us)
Async XLA Ops:
  0.0 26.2 %collective-permute-start = (bf16[64,4096]{1,0:T(8,128)(2,1)}, bf16[64,4096]{1,0:T(8,128)(2,1)S(1)}, u32[]{:S(2)}, u32[]{:S(2)}) collective-permute-start(bf16[64,4096]{1,0:T(8,128)(2,1)} %bitcast.60), channel_id=1, source_target_pairs={{16,0},{0,16},{17,1},{1,17},{18,2},{2,18},{19,3},{3,19},{20,4},{4,... | collective-permute-start | bytes 1572872 | tf_op jit(solution)/shard_map/ppermute | solution.py:36
  3.7 21.8 %collective-permute-start.1 = (bf16[64,128]{1,0:T(8,128)(2,1)S(1)}, bf16[64,128]{1,0:T(8,128)(2,1)S(1)}, u32[]{:S(2)}, u32[]{:S(2)}) collective-permute-start(bf16[64,128]{1,0:T(8,128)(2,1)S(1)} %convert_bitcast_fusion), channel_id=1, source_target_pairs={{16,0},{0,16},{17,1},{1,17},{18,2},{2,18},{19,3},{3,19},{20,4},{4,... | collective-permute-start | bytes 49160 | tf_op jit(solution)/shard_map/ppermute | solution.py:36
  4.6 50.6 %collective-permute-start.2 = (bf16[64,256]{0,1:T(8,128)(2,1)S(1)}, bf16[64,256]{0,1:T(8,128)(2,1)S(1)}, u32[]{:S(2)}, u32[]{:S(2)}) collective-permute-start(bf16[64,256]{0,1:T(8,128)(2,1)S(1)} %bitcast.59), channel_id=1, source_target_pairs={{16,0},{0,16},{17,1},{1,17},{18,2},{2,18},{19,3},{3,19},{20,4},{4,... | collective-permute-start | bytes 98312 | tf_op jit(solution)/shard_map/ppermute | solution.py:36
  7.4 47.8 %collective-permute-start.3 = (bf16[64,8]{0,1:T(8,128)(2,1)S(1)}, bf16[64,8]{0,1:T(8,128)(2,1)S(1)}, u32[]{:S(2)}, u32[]{:S(2)}) collective-permute-start(bf16[64,8]{0,1:T(8,128)(2,1)S(1)} %convert_bitcast_fusion.2), channel_id=1, source_target_pairs={{16,0},{0,16},{17,1},{1,17},{18,2},{2,18},{19,3},{3,19},{20,4},{4,... | collective-permute-start | bytes 3080 | tf_op jit(solution)/shard_map/ppermute | solution.py:36
  8.3 61.9 %collective-permute-start.4 = (bf16[64,256]{0,1:T(8,128)(2,1)S(1)}, bf16[64,256]{0,1:T(8,128)(2,1)S(1)}, u32[]{:S(2)}, u32[]{:S(2)}) collective-permute-start(bf16[64,256]{0,1:T(8,128)(2,1)S(1)} %bitcast.58), channel_id=1, source_target_pairs={{16,0},{0,16},{17,1},{1,17},{18,2},{2,18},{19,3},{3,19},{20,4},{4,... | collective-permute-start | bytes 98312 | tf_op jit(solution)/shard_map/ppermute | solution.py:36
  25.5 29.7 %collective-permute-start.5 = (bf16[64,8]{0,1:T(8,128)(2,1)S(1)}, bf16[64,8]{0,1:T(8,128)(2,1)S(1)}, u32[]{:S(2)}, u32[]{:S(2)}) collective-permute-start(bf16[64,8]{0,1:T(8,128)(2,1)S(1)} %convert_bitcast_fusion.1), channel_id=1, source_target_pairs={{16,0},{0,16},{17,1},{1,17},{18,2},{2,18},{19,3},{3,19},{20,4},{4,... | collective-permute-start | bytes 3080 | tf_op jit(solution)/shard_map/ppermute | solution.py:36
  26.7 5.9 %copy-start.6 = (bf16[1,2,128,128]{3,2,1,0:T(8,128)(2,1)S(1)}, bf16[1,2,128,128]{3,2,1,0:T(8,128)(2,1)}, u32[]{:S(2)}) copy-start(bf16[1,2,128,128]{3,2,1,0:T(8,128)(2,1)} %param.22) | copy-start | bytes 196612
  28.0 57.0 %all-to-all-start = ((bf16[64,32,128]{2,0,1:T(8,128)(2,1)}), bf16[64,32,128]{2,0,1:T(8,128)(2,1)S(1)}, u32[]{:S(2)}, u32[]{:S(2)}) async-start(bf16[64,32,128]{2,0,1:T(8,128)(2,1)} %copy.39), calls=%async_computation | async-start | bytes 1048576 | tf_op jit(solution)/shard_map/all_to_all | solution.py:145
  88.4 1.3 %copy-start = (bf16[8,512,128]{2,1,0:T(8,128)(2,1)S(1)}, bf16[8,512,128]{2,1,0:T(8,128)(2,1)}, u32[]{:S(2)}) copy-start(bf16[8,512,128]{2,1,0:T(8,128)(2,1)} %get-tuple-element.165) | copy-start | bytes 3145732 | tf_op jit(solution)/shard_map/while/body/eval_jaxpr/cond
  88.4 1.5 %copy-start.1 = (f32[8,256,128]{2,1,0:T(8,128)S(1)}, f32[8,256,128]{2,1,0:T(8,128)}, u32[]{:S(2)}) copy-start(f32[8,256,128]{2,1,0:T(8,128)} %get-tuple-element.162) | copy-start | bytes 3145732 | tf_op jit(solution)/shard_map/while/body/eval_jaxpr/cond
  91.6 1.0 copy-start.2
  92.6 1.2 %copy-start.3 = (f32[8,256,128]{2,1,0:T(8,128)S(1)}, f32[8,256,128]{2,1,0:T(8,128)}, u32[]{:S(2)}) copy-start(f32[8,256,128]{2,1,0:T(8,128)} %get-tuple-element.147) | copy-start | bytes 3145732
  92.6 1.4 %copy-start.5 = (bf16[8,256,128]{2,1,0:T(8,128)(2,1)S(1)}, bf16[8,256,128]{2,1,0:T(8,128)(2,1)}, u32[]{:S(2)}) copy-start(bf16[8,256,128]{2,1,0:T(8,128)(2,1)} %gather_fusion.3) | copy-start | bytes 1572868
  95.4 0.8 copy-start.4
  96.3 5.5 %collective-permute-start.6 = (bf16[64,8,128]{2,0,1:T(8,128)(2,1)S(1)}, bf16[64,8,128]{2,0,1:T(8,128)(2,1)S(1)}, u32[]{:S(2)}, u32[]{:S(2)}) collective-permute-start(bf16[64,8,128]{2,0,1:T(8,128)(2,1)S(1)} %get-tuple-element.186), channel_id=1, source_target_pairs={{0,4},{4,0},{8,12},{12,8},{1,5},{5,1},{9,13},{13,9},{2,6},{6,2},{1... | collective-permute-start | bytes 393224 | tf_op jit(solution)/shard_map/ppermute | solution.py:23
  97.2 7.3 %collective-permute-start.7 = (bf16[64,8,128]{2,0,1:T(8,128)(2,1)S(1)}, bf16[64,8,128]{2,0,1:T(8,128)(2,1)S(1)}, u32[]{:S(2)}, u32[]{:S(2)}) collective-permute-start(bf16[64,8,128]{2,0,1:T(8,128)(2,1)S(1)} %get-tuple-element.185), channel_id=1, source_target_pairs={{0,8},{4,12},{8,0},{12,4},{1,9},{5,13},{9,1},{13,5},{2,10},{6,14},... | collective-permute-start | bytes 393224 | tf_op jit(solution)/shard_map/ppermute | solution.py:23
  99.6 6.9 %collective-permute-start.8 = (bf16[64,8,128]{2,0,1:T(8,128)(2,1)S(1)}, bf16[64,8,128]{2,0,1:T(8,128)(2,1)S(1)}, u32[]{:S(2)}, u32[]{:S(2)}) collective-permute-start(bf16[64,8,128]{2,0,1:T(8,128)(2,1)S(1)} %get-tuple-element.184), channel_id=1, source_target_pairs={{0,12},{4,8},{8,4},{12,0},{1,13},{5,9},{9,5},{13,1},{2,14},{6,10},... | collective-permute-start | bytes 393224 | tf_op jit(solution)/shard_map/ppermute | solution.py:23
